TPU v7x, 32 devices: a whole 2x2x4 slice. The times are simulated.
32 devices in a mesh: pipe: 2 (over core), dp: 16 (over z, y, x).
Axes of the slice: x: 2, y: 2, z: 4, core: 2. Of those that a mesh axis runs over, the one named last changes fastest.
Arguments:
- feats: bfloat16 [256, 8, 10, 768], P('dp'), may hold values from -6 to 6
- dw_kernel: bfloat16 [2, 7, 7, 768], P('pipe'), may hold values from -0.875 to 0.875
- ln_gain: float32 [2, 768], P('pipe'), may hold values from 0.25 to 1.75
- w_in: bfloat16 [2, 768, 3072], P('pipe'), may hold values from -0.21875 to 0.21875
- w_out: bfloat16 [2, 3072, 768], P('pipe'), may hold values from -0.109375 to 0.109375
- layer_scale: float32 [2, 768], P('pipe'), may hold values from 0.3 to 3
- head_gain: float32 [768], replicated, may hold values from 0.25 to 1.75
- head_proj: bfloat16 [768, 1024], replicated, may hold values from -0.21875 to 0.21875
- yield_embeds: bfloat16 [2048, 1024], P(('pipe', 'dp')), may hold values from -0.19921875 to 0.19921875
- match_ids: int32 [256], P('dp'), may hold values from 0 to 2047
- logit_scale: float32 [], replicated, may hold values from 5 to 20
- logit_bias: float32 [], replicated, may hold values from -4 to -1
Outputs:
- projected: bfloat16 [256, 1024], P('dp')
- embed_grad: float32 [256, 1024], P('dp')
Inputs may be any that keep to these rules, and one draw needn't show every extreme that they name: `match_ids`: index of the yield embedding paired with each image.
All inputs are finite; a program needn't handle non-finite values.
Results may differ from a plain program's by a relative error of at most 0.015.
Values may be sent and summed in bfloat16 or wider, within the bound.
A program may use at most 128 MiB of HBM per device.

v0:
```python
import jax
import jax.numpy as jnp
from jax import lax
from jax.sharding import PartitionSpec as P

MICRO_IMG = 4


def shifted(value, axis, steps):
    count = lax.axis_size(axis)
    initial, last = (max(0, -steps), min(count, count - steps))
    return lax.ppermute(value, axis, [(source, source + steps) for source in range(initial, last)])


def from_root(block, axis, holder):
    block = jnp.where(lax.axis_index(axis) == holder, block, jnp.zeros_like(block))
    return lax.psum(block, axis)


def layer_norm(value, gain):
    mean = jnp.mean(value, axis=-1, keepdims=True)
    centred = value - mean
    var = jnp.mean(centred * centred, axis=-1, keepdims=True)
    return centred * lax.rsqrt(var + 1e-06) * gain


def depthwise_batch(act, kernel):
    rows = act.shape[1]
    cols = act.shape[2]
    padded = jnp.pad(act.astype(jnp.float32), ((0, 0), (3, 3), (3, 3), (0, 0)))
    kernel32 = kernel.astype(jnp.float32)
    total = jnp.zeros(act.shape, jnp.float32)
    for row_off in range(7):
        for col_off in range(7):
            total = (
                total
                + padded[:, row_off : row_off + rows, col_off : col_off + cols, :]
                * kernel32[row_off, col_off]
            )
    return total


def block_batch(act, kernel, gain, weight_in, weight_out, scale):
    channels = act.shape[-1]
    conv = depthwise_batch(act, kernel)
    normed = layer_norm(conv, gain).astype(jnp.bfloat16).reshape(-1, channels)
    hidden = jax.nn.gelu(
        jnp.dot(normed, weight_in, preferred_element_type=jnp.float32), approximate=False
    ).astype(jnp.bfloat16)
    branch = jnp.dot(hidden, weight_out, preferred_element_type=jnp.float32)
    result = act.reshape(-1, channels).astype(jnp.float32) + scale * branch
    return result.astype(jnp.bfloat16).reshape(act.shape)


def pair_terms(unit_rows, match_rows, yield_rows, first_global, logit_scale, logit_bias):
    logits = (
        logit_scale * jnp.dot(unit_rows, yield_rows.T, preferred_element_type=jnp.float32)
        + logit_bias
    )
    columns = first_global + jnp.arange(yield_rows.shape[0], dtype=jnp.int32)
    label = jnp.where(match_rows[:, None] == columns[None, :], 1.0, -1.0).astype(jnp.float32)
    coef = (-label * logit_scale * jax.nn.sigmoid(-label * logits)).astype(jnp.bfloat16)
    return jnp.dot(coef, yield_rows, preferred_element_type=jnp.float32)


def on_device(
    feats,
    dw_kernel,
    ln_gain,
    w_in,
    w_out,
    layer_scale,
    head_gain,
    head_proj,
    yield_embeds,
    match_ids,
    logit_scale,
    logit_bias,
):
    sections = lax.axis_size("pipe")
    segment = lax.axis_index("pipe")
    images = feats.shape[0]
    group = MICRO_IMG
    batches = images // group
    channels = feats.shape[-1]

    def run_block(act):
        return block_batch(act, dw_kernel[0], ln_gain[0], w_in[0], w_out[0], layer_scale[0])

    def skip_block(act):
        return jnp.zeros_like(act)

    def tick(step, carry):
        incoming, pooled = carry
        slot = step - segment
        valid = jnp.logical_and(slot >= 0, slot < batches)
        position = jnp.clip(slot, 0, batches - 1)
        fresh = lax.dynamic_slice_in_dim(feats, position * group, group, 0)
        source = jnp.where(segment == 0, fresh, incoming)
        result = lax.cond(valid, run_block, skip_block, source)
        mean_rows = jnp.mean(result.astype(jnp.float32), axis=(1, 2))
        keep = jnp.logical_and(valid, segment == sections - 1)
        updated = lax.dynamic_update_slice(pooled, mean_rows, (position * group, 0))
        pooled = jnp.where(keep, updated, pooled)
        incoming = shifted(result, "pipe", 1)
        return (incoming, pooled)

    start_carry = (
        jnp.zeros((group,) + feats.shape[1:], jnp.bfloat16),
        jnp.zeros((images, channels), jnp.float32),
    )
    unused, pooled = lax.fori_loop(0, batches + sections - 1, tick, start_carry)
    head_normed = layer_norm(pooled, head_gain).astype(jnp.bfloat16)
    local_proj = jnp.dot(head_normed, head_proj, preferred_element_type=jnp.float32).astype(
        jnp.bfloat16
    )
    projected = from_root(local_proj, "pipe", sections - 1)
    wide = projected.astype(jnp.float32)
    unit = (wide / jnp.sqrt(jnp.sum(wide * wide, axis=-1, keepdims=True) + 1e-06)).astype(
        jnp.bfloat16
    )
    owners = lax.axis_size("dp")
    block_rows = yield_embeds.shape[0]
    row_base = segment * owners * block_rows
    partial_grad = pair_terms(
        unit,
        match_ids,
        lax.all_gather(yield_embeds, "dp", axis=0, tiled=True),
        row_base,
        logit_scale,
        logit_bias,
    )
    embed_grad = lax.psum(partial_grad.astype(jnp.bfloat16), "pipe").astype(jnp.float32)
    return (projected, embed_grad)


def solution(mesh):
    in_specs = (
        P("dp", None, None, None),
        P("pipe", None, None, None),
        P("pipe", None),
        P("pipe", None, None),
        P("pipe", None, None),
        P("pipe", None),
        P(),
        P(),
        P(("pipe", "dp"), None),
        P("dp"),
        P(),
        P(),
    )
    out_specs = (P("dp", None), P("dp", None))
    return jax.shard_map(
        on_device, mesh=mesh, in_specs=in_specs, out_specs=out_specs, check_vma=False
    )
```

profile of v0, /device:TPU:0, one launch (start us, length us, event | category | flops | bytes accessed | tf_op | source)
XLA Modules:
  0.0 365.1 jit_solution(296075181988076223)
XLA Ops:
  7.9 3.9 %copy.18 = bf16[16,8,10,768]{3,2,1,0:T(8,128)(2,1)} copy(bf16[16,8,10,768]{3,1,2,0:T(8,128)(2,1)} %param.16) | data formatting | bytes 3932160 | tf_op jit(solution)/shard_map/while | solution.py:112
  12.5 330.3 %while.16 = (s32[]{:T(128)}, bf16[4,8,10,768]{3,1,2,0:T(8,128)(2,1)S(1)}, f32[16,768]{1,0:T(8,128)}, s32[]{:T(128)}, pred[]{:T(512)}, /*index=5*/bf16[16,8,10,76...) while((s32[]{:T(128)}, ...), condition=%wide.region_6.7_spmd, body=%wide.region_0.6_spmd.sunk | while | flops 3111362560 | bytes 25923224 | solution.py:112
  12.5 61.2 %conditional.2 = (bf16[4,8,10,768]{3,2,1,0:T(8,128)(2,1)}, f32[4,768]{1,0:T(4,128)S(1)}) conditional(s32[]{:T(128)} %convert_element_type.115, () %tuple.101, (pred[]{:T(512)}, bf16[16,8,10,768]{3,2,1,0:T(8,128)(2,1)}, s32[]{:T(128)}, bf16[4,8,10,768]{3,1,2,0:T(8,128)(2,1)S(1)}, f32[1,768]{1,0:T(1,128)S(1)}, ...), branch_computations={%region_1.1_spmd, %region_2.5_spmd} | conditional | flops 3111356416 | bytes 22936348 | solution.py:100
  13.8 2.5 fusion.166
  16.3 35.3 %fusion.227 = (f32[4,8,10]{2,1,0:T(8,128)S(1)}, f32[4,8,10,768]{3,2,1,0:T(8,128)S(1)}) fusion(f32[768]{0:T(1024)S(1)} %get-tuple-element.324, f32[768]{0:T(1024)S(1)} %get-tuple-element.325, f32[768]{0:T(1024)S(1)} %get-tuple-element.326, f32[768]{0:T(1024)S(1)} %get-tuple-element.327, f32[768]{0:T(1024)S(1)} %get-tuple-element.328, ...), kind=kLoop, calls=%fused_computation.326 | loop fusion | flops 24084160 | bytes 2117888 | tf_op jit(solution)/shard_map/while/body/eval_jaxpr/cond/branch_1_fun/reduce_sum | solution.py:21
  56.7 14.6 %fusion.159 = bf16[320,768]{1,0:T(8,128)(2,1)S(1)} fusion(f32[320,768]{1,0:T(8,128)S(1)} %reshape.104, bf16[1,3072,768]{2,1,0:T(8,128)(2,1)} %get-tuple-element.258, bf16[320,768]{1,0:T(8,128)(2,1)S(1)} %reshape.102, bf16[1,768,3072]{2,1,0:T(8,128)(2,1)} %get-tuple-element.257, f32[768]{0:T(1024)S(1)} %reduce), kind=kOutput, calls=%fused_computation.202 | convolution fusion | flops 3084533760 | bytes 11406336 | tf_op jit(solution)/shard_map/while/body/eval_jaxpr/cond/branch_1_fun/dot_general | solution.py:50
  77.8 61.2 %conditional.2 = (bf16[4,8,10,768]{3,2,1,0:T(8,128)(2,1)}, f32[4,768]{1,0:T(4,128)S(1)}) conditional(s32[]{:T(128)} %convert_element_type.115, () %tuple.101, (pred[]{:T(512)}, bf16[16,8,10,768]{3,2,1,0:T(8,128)(2,1)}, s32[]{:T(128)}, bf16[4,8,10,768]{3,1,2,0:T(8,128)(2,1)S(1)}, f32[1,768]{1,0:T(1,128)S(1)}, ...), branch_computations={%region_1.1_spmd, %region_2.5_spmd} | conditional | flops 3111356416 | bytes 22936348 | solution.py:100
  79.1 2.5 fusion.166
  81.6 35.3 %fusion.227 = (f32[4,8,10]{2,1,0:T(8,128)S(1)}, f32[4,8,10,768]{3,2,1,0:T(8,128)S(1)}) fusion(f32[768]{0:T(1024)S(1)} %get-tuple-element.324, f32[768]{0:T(1024)S(1)} %get-tuple-element.325, f32[768]{0:T(1024)S(1)} %get-tuple-element.326, f32[768]{0:T(1024)S(1)} %get-tuple-element.327, f32[768]{0:T(1024)S(1)} %get-tuple-element.328, ...), kind=kLoop, calls=%fused_computation.326 | loop fusion | flops 24084160 | bytes 2117888 | tf_op jit(solution)/shard_map/while/body/eval_jaxpr/cond/branch_1_fun/reduce_sum | solution.py:21
  122.0 14.6 %fusion.159 = bf16[320,768]{1,0:T(8,128)(2,1)S(1)} fusion(f32[320,768]{1,0:T(8,128)S(1)} %reshape.104, bf16[1,3072,768]{2,1,0:T(8,128)(2,1)} %get-tuple-element.258, bf16[320,768]{1,0:T(8,128)(2,1)S(1)} %reshape.102, bf16[1,768,3072]{2,1,0:T(8,128)(2,1)} %get-tuple-element.257, f32[768]{0:T(1024)S(1)} %reduce), kind=kOutput, calls=%fused_computation.202 | convolution fusion | flops 3084533760 | bytes 11406336 | tf_op jit(solution)/shard_map/while/body/eval_jaxpr/cond/branch_1_fun/dot_general | solution.py:50
  140.3 2.3 collective-permute-start
  144.0 61.2 %conditional.2 = (bf16[4,8,10,768]{3,2,1,0:T(8,128)(2,1)}, f32[4,768]{1,0:T(4,128)S(1)}) conditional(s32[]{:T(128)} %convert_element_type.115, () %tuple.101, (pred[]{:T(512)}, bf16[16,8,10,768]{3,2,1,0:T(8,128)(2,1)}, s32[]{:T(128)}, bf16[4,8,10,768]{3,1,2,0:T(8,128)(2,1)S(1)}, f32[1,768]{1,0:T(1,128)S(1)}, ...), branch_computations={%region_1.1_spmd, %region_2.5_spmd} | conditional | flops 3111356416 | bytes 22936348 | solution.py:100
  145.4 2.5 fusion.166
  147.9 35.3 %fusion.227 = (f32[4,8,10]{2,1,0:T(8,128)S(1)}, f32[4,8,10,768]{3,2,1,0:T(8,128)S(1)}) fusion(f32[768]{0:T(1024)S(1)} %get-tuple-element.324, f32[768]{0:T(1024)S(1)} %get-tuple-element.325, f32[768]{0:T(1024)S(1)} %get-tuple-element.326, f32[768]{0:T(1024)S(1)} %get-tuple-element.327, f32[768]{0:T(1024)S(1)} %get-tuple-element.328, ...), kind=kLoop, calls=%fused_computation.326 | loop fusion | flops 24084160 | bytes 2117888 | tf_op jit(solution)/shard_map/while/body/eval_jaxpr/cond/branch_1_fun/reduce_sum | solution.py:21
  188.3 14.6 %fusion.159 = bf16[320,768]{1,0:T(8,128)(2,1)S(1)} fusion(f32[320,768]{1,0:T(8,128)S(1)} %reshape.104, bf16[1,3072,768]{2,1,0:T(8,128)(2,1)} %get-tuple-element.258, bf16[320,768]{1,0:T(8,128)(2,1)S(1)} %reshape.102, bf16[1,768,3072]{2,1,0:T(8,128)(2,1)} %get-tuple-element.257, f32[768]{0:T(1024)S(1)} %reduce), kind=kOutput, calls=%fused_computation.202 | convolution fusion | flops 3084533760 | bytes 11406336 | tf_op jit(solution)/shard_map/while/body/eval_jaxpr/cond/branch_1_fun/dot_general | solution.py:50
  210.3 61.2 %conditional.2 = (bf16[4,8,10,768]{3,2,1,0:T(8,128)(2,1)}, f32[4,768]{1,0:T(4,128)S(1)}) conditional(s32[]{:T(128)} %convert_element_type.115, () %tuple.101, (pred[]{:T(512)}, bf16[16,8,10,768]{3,2,1,0:T(8,128)(2,1)}, s32[]{:T(128)}, bf16[4,8,10,768]{3,1,2,0:T(8,128)(2,1)S(1)}, f32[1,768]{1,0:T(1,128)S(1)}, ...), branch_computations={%region_1.1_spmd, %region_2.5_spmd} | conditional | flops 3111356416 | bytes 22936348 | solution.py:100
  211.6 2.5 fusion.166
  214.1 35.3 %fusion.227 = (f32[4,8,10]{2,1,0:T(8,128)S(1)}, f32[4,8,10,768]{3,2,1,0:T(8,128)S(1)}) fusion(f32[768]{0:T(1024)S(1)} %get-tuple-element.324, f32[768]{0:T(1024)S(1)} %get-tuple-element.325, f32[768]{0:T(1024)S(1)} %get-tuple-element.326, f32[768]{0:T(1024)S(1)} %get-tuple-element.327, f32[768]{0:T(1024)S(1)} %get-tuple-element.328, ...), kind=kLoop, calls=%fused_computation.326 | loop fusion | flops 24084160 | bytes 2117888 | tf_op jit(solution)/shard_map/while/body/eval_jaxpr/cond/branch_1_fun/reduce_sum | solution.py:21
  254.5 14.6 %fusion.159 = bf16[320,768]{1,0:T(8,128)(2,1)S(1)} fusion(f32[320,768]{1,0:T(8,128)S(1)} %reshape.104, bf16[1,3072,768]{2,1,0:T(8,128)(2,1)} %get-tuple-element.258, bf16[320,768]{1,0:T(8,128)(2,1)S(1)} %reshape.102, bf16[1,768,3072]{2,1,0:T(8,128)(2,1)} %get-tuple-element.257, f32[768]{0:T(1024)S(1)} %reduce), kind=kOutput, calls=%fused_computation.202 | convolution fusion | flops 3084533760 | bytes 11406336 | tf_op jit(solution)/shard_map/while/body/eval_jaxpr/cond/branch_1_fun/dot_general | solution.py:50
  272.8 2.3 collective-permute-start
  278.8 62.5 %collective-permute-start = (bf16[4,8,10,768]{3,1,2,0:T(8,128)(2,1)S(1)}, bf16[4,8,10,768]{3,1,2,0:T(8,128)(2,1)S(1)}, u32[]{:S(2)}, u32[]{:S(2)}) collective-permute-start(bf16[4,8,10,768]{3,1,2,0:T(8,128)(2,1)S(1)} %copy.23), channel_id=1, source_target_pairs={{0,16},{1,17},{2,18},{3,19},{4,20},{5,21},{6,22},{7,23},{8,24},{9,... | collective-permute-start | bytes 1474568 | tf_op jit(solution)/shard_map/while/body/eval_jaxpr/ppermute | solution.py:12
  347.2 3.6 psum.14
  351.0 3.2 convolution_convert_fusion.1
  354.2 3.4 psum.15
  (98 shorter events, 59.4 us)
Async XLA Ops:
  7.2 338.9 %copy-start = (bf16[768,1024]{1,0:T(8,128)(2,1)S(1)}, bf16[768,1024]{1,0:T(8,128)(2,1)}, u32[]{:S(2)}) copy-start(bf16[768,1024]{1,0:T(8,128)(2,1)} %param.23) | copy-start | bytes 4718596
  7.2 343.8 %all-gather.2.cloned.1.call-start = ((), (), s32[]{:S(2)}) async-start(), calls=%async_computation | async-start | bytes 2228224 | tf_op jit(solution)/shard_map/all_gather | solution.py:128
  7.9 4.6 %copy-start.2 = (f32[1,768]{1,0:T(1,128)S(1)}, f32[1,768]{1,0:T(1,128)}, u32[]{:S(2)}) copy-start(f32[1,768]{1,0:T(1,128)} %param.21) | copy-start | bytes 9220
  75.0 2.8 collective-permute-start
  140.3 3.8 %collective-permute-start = (bf16[4,8,10,768]{3,1,2,0:T(8,128)(2,1)S(1)}, bf16[4,8,10,768]{3,1,2,0:T(8,128)(2,1)S(1)}, u32[]{:S(2)}, u32[]{:S(2)}) collective-permute-start(bf16[4,8,10,768]{3,1,2,0:T(8,128)(2,1)S(1)} %copy.23), channel_id=1, source_target_pairs={{0,16},{1,17},{2,18},{3,19},{4,20},{5,21},{6,22},{7,23},{8,24},{9,... | collective-permute-start | bytes 1474568 | tf_op jit(solution)/shard_map/while/body/eval_jaxpr/ppermute | solution.py:12
  206.5 3.8 %collective-permute-start = (bf16[4,8,10,768]{3,1,2,0:T(8,128)(2,1)S(1)}, bf16[4,8,10,768]{3,1,2,0:T(8,128)(2,1)S(1)}, u32[]{:S(2)}, u32[]{:S(2)}) collective-permute-start(bf16[4,8,10,768]{3,1,2,0:T(8,128)(2,1)S(1)} %copy.23), channel_id=1, source_target_pairs={{0,16},{1,17},{2,18},{3,19},{4,20},{5,21},{6,22},{7,23},{8,24},{9,... | collective-permute-start | bytes 1474568 | tf_op jit(solution)/shard_map/while/body/eval_jaxpr/ppermute | solution.py:12
  272.8 3.8 %collective-permute-start = (bf16[4,8,10,768]{3,1,2,0:T(8,128)(2,1)S(1)}, bf16[4,8,10,768]{3,1,2,0:T(8,128)(2,1)S(1)}, u32[]{:S(2)}, u32[]{:S(2)}) collective-permute-start(bf16[4,8,10,768]{3,1,2,0:T(8,128)(2,1)S(1)} %copy.23), channel_id=1, source_target_pairs={{0,16},{1,17},{2,18},{3,19},{4,20},{5,21},{6,22},{7,23},{8,24},{9,... | collective-permute-start | bytes 1474568 | tf_op jit(solution)/shard_map/while/body/eval_jaxpr/ppermute | solution.py:12
  278.8 64.0 %collective-permute-start = (bf16[4,8,10,768]{3,1,2,0:T(8,128)(2,1)S(1)}, bf16[4,8,10,768]{3,1,2,0:T(8,128)(2,1)S(1)}, u32[]{:S(2)}, u32[]{:S(2)}) collective-permute-start(bf16[4,8,10,768]{3,1,2,0:T(8,128)(2,1)S(1)} %copy.23), channel_id=1, source_target_pairs={{0,16},{1,17},{2,18},{3,19},{4,20},{5,21},{6,22},{7,23},{8,24},{9,... | collective-permute-start | bytes 1474568 | tf_op jit(solution)/shard_map/while/body/eval_jaxpr/ppermute | solution.py:12
  342.8 8.2 %copy-start.3 = (s32[16]{0:T(128)S(1)}, s32[16]{0:T(128)}, u32[]{:S(2)}) copy-start(s32[16]{0:T(128)} %param.25) | copy-start | bytes 196
  350.8 3.4 copy-start.1
Sparse Core Ops, SparseCore 0:
  10.8 63.4 all-gather.1
where the time goes:
time: 368 us; the launch traced here: 365 us
  other arithmetic  178 us (48%)
  starting transfers between devices  70.8 us (19%)
  matrix products  62.8 us (17%)
  local copies, waits for them, and re-layouts  29.4 us (8%)
  between operations  15.4 us (4%)
  blocking collectives  7.01 us (2%)
    reduce_sum x5, other arithmetic, layer_norm(): mean = jnp.mean(value, axis=-1, keepdims=True)  142 us
    ppermute x5, starting transfers between devices, shifted(): lax.ppermute(value, axis, [(source, source + steps) for source in range(i...  70.8 us
    dot_general x4, matrix products, block_batch(): branch = jnp.dot(hidden, weight_out, preferred_element_type=jnp.float32)  58.5 us
    convert_element_type x4, other arithmetic, block_batch(): result = act.reshape(-1, channels).astype(jnp.float32) + scale * branch  10.1 us
  transfers between devices with their start and end apart: 6, of which 5 were waited for; matrix products, arithmetic and copies ran while one was open for 73% of the time, Pallas kernels for 0%

commit v1 on v0

v1 whole, which is shorter than its diff:
```python
import functools

import jax
import jax.numpy as jnp
from jax import lax
from jax.experimental import pallas as pl
from jax.experimental.pallas import tpu as pltpu
from jax.sharding import PartitionSpec as P

CHUNK = 256
LANES = 128
ERF_POLY = (
    7.97872669e-01,
    3.63655561e-02,
    -5.77947342e-05,
    -4.72814832e-05,
    2.79985521e-06,
    -5.66473023e-08,
)
ERF_EDGE = 5.5 * 5.5


def gelu(x):
    x2 = jnp.minimum(x * x, ERF_EDGE)
    poly = ERF_POLY[-1]
    for coefficient in ERF_POLY[-2::-1]:
        poly = poly * x2 + coefficient
    half = 0.5 * x
    return half + half * jnp.tanh(x * poly)


def normalise(value, gain):
    mean = jnp.mean(value, axis=-1, keepdims=True)
    centred = value - mean
    var = jnp.mean(centred * centred, axis=-1, keepdims=True)
    return centred * lax.rsqrt(var + 1e-06) * gain


def tower_kernel(
    taps,
    feats_hbm,
    small_hbm,
    win_hbm,
    wout_hbm,
    hgain_ref,
    hproj_ref,
    out_ref,
    feats,
    small,
    win,
    wout,
    act,
    conv,
    normed,
    acc,
    raw_a,
    raw_b,
    wide_taps,
    proj,
    feat_sem,
    small_sem,
    in_sem,
    out_sem,
    small_send,
    in_send,
    out_send,
    proj_send,
    proj_recv,
):
    images, rows, cols, channels = feats.shape
    sections = win.shape[0]
    chunks = win.shape[1]
    places = rows * cols
    reach = taps // 2
    me = lax.axis_index("pipe")
    other = 1 - me
    peer = {"pipe": other}

    def in_source(c):
        return win_hbm.at[:, pl.ds(pl.multiple_of(c * CHUNK, CHUNK), CHUNK)]

    def out_source(c):
        return wout_hbm.at[pl.ds(pl.multiple_of(c * CHUNK, CHUNK), CHUNK), :]

    def local_small():
        return pltpu.make_async_copy(small_hbm, small.at[me], small_sem.at[me])

    def local_in(c):
        return pltpu.make_async_copy(in_source(c), win.at[me, c], in_sem.at[me, c])

    def local_out(c):
        return pltpu.make_async_copy(out_source(c), wout.at[me, c], out_sem.at[me, c])

    def remote(source, target, send, recv):
        return pltpu.make_async_remote_copy(
            src_ref=source,
            dst_ref=target,
            send_sem=send,
            recv_sem=recv,
            device_id=peer,
            device_id_type=pl.DeviceIdType.MESH,
        )

    def remote_small(section):
        return remote(small_hbm, small.at[section], small_send, small_sem.at[section])

    def remote_in(section, c):
        return remote(in_source(c), win.at[section, c], in_send.at[c], in_sem.at[section, c])

    def remote_out(section, c):
        return remote(out_source(c), wout.at[section, c], out_send.at[c], out_sem.at[section, c])

    fetch = pltpu.make_async_copy(feats_hbm.at[pl.ds(me * images, images)], feats, feat_sem)
    fetch.start()
    local_small().start()

    barrier = pltpu.get_barrier_semaphore()
    pl.semaphore_signal(barrier, inc=1, device_id=peer, device_id_type=pl.DeviceIdType.MESH)
    pl.semaphore_wait(barrier, 1)

    remote_small(me).start()

    def begin(c, carry):
        remote_in(me, c).start()
        local_in(c).start()
        remote_out(me, c).start()
        local_out(c).start()
        return carry

    lax.fori_loop(0, chunks, begin, 0)

    def await_small(section):
        @pl.when(section == me)
        def _():
            local_small().wait()

        @pl.when(section != me)
        def _():
            remote_small(section).wait_recv()

    def await_chunk(section, c):
        @pl.when(section == me)
        def _():
            local_in(c).wait()
            local_out(c).wait()

        @pl.when(section != me)
        def _():
            remote_in(section, c).wait_recv()
            remote_out(section, c).wait_recv()

    fetch.wait()

    def spread(image, carry):
        for r in range(rows):
            line = feats[image, r].astype(jnp.float32)
            for block in range(channels // LANES):
                act[block, pl.ds(r * cols * images + image, cols, stride=images), :] = line[
                    :, block * LANES : (block + 1) * LANES
                ]
        return carry

    for image in range(images):
        spread(image, 0)

    def one_section(section, carry):
        await_small(section)

        def conv_lanes(block, inner):
            lanes = pl.ds(pl.multiple_of(block * LANES, LANES), LANES)
            for k in range(taps * taps):
                wide_taps[k] = jnp.broadcast_to(small[section, pl.ds(k, 1), lanes], (images, LANES))
            for r in range(rows):
                total = [None] * cols
                for dy in range(taps):
                    source = r + dy - reach
                    if not 0 <= source < rows:
                        continue
                    kernel = [wide_taps[dy * taps + dx] for dx in range(taps)]
                    line = [
                        act[block, pl.ds((source * cols + w) * images, images), :]
                        for w in range(cols)
                    ]
                    for w in range(cols):
                        for dx in range(taps):
                            at = w + dx - reach
                            if not 0 <= at < cols:
                                continue
                            term = line[at] * kernel[dx]
                            total[w] = term if total[w] is None else total[w] + term
                for w in range(cols):
                    conv[pl.ds((r * cols + w) * images, images), lanes] = total[w]
            return inner

        lax.fori_loop(0, channels // LANES, conv_lanes, 0)

        gain = small[section, pl.ds(taps * taps, 1), :]
        step_rows = 32

        def norm_rows(block, inner):
            at = pl.ds(pl.multiple_of(block * step_rows, step_rows), step_rows)
            normed[at, :] = normalise(conv[at, :], gain).astype(jnp.bfloat16)
            return inner

        lax.fori_loop(0, places * images // step_rows, norm_rows, 0, unroll=4)

        acc[...] = jnp.zeros_like(acc)
        await_chunk(section, 0)
        raw_a[...] = jnp.dot(normed[...], win[section, 0], preferred_element_type=jnp.float32)

        def pair(j, inner):
            first = 2 * j
            after = jnp.minimum(first + 2, chunks - 1)
            await_chunk(section, first + 1)

            @pl.when(first + 2 < chunks)
            def _():
                await_chunk(section, after)

            raw_b[...] = jnp.dot(
                normed[...], win[section, first + 1], preferred_element_type=jnp.float32
            )
            acc[...] += jnp.dot(
                gelu(raw_a[...]).astype(jnp.bfloat16),
                wout[section, first],
                preferred_element_type=jnp.float32,
            )
            raw_a[...] = jnp.dot(
                normed[...], win[section, after], preferred_element_type=jnp.float32
            )
            acc[...] += jnp.dot(
                gelu(raw_b[...]).astype(jnp.bfloat16),
                wout[section, first + 1],
                preferred_element_type=jnp.float32,
            )
            return inner

        lax.fori_loop(0, chunks // 2, pair, 0)

        scale = small[section, pl.ds(taps * taps + 1, 1), :]

        def add_rows(block, inner):
            at = pl.ds(pl.multiple_of(block * step_rows, step_rows), step_rows)
            for lane in range(channels // LANES):
                lanes = slice(lane * LANES, (lane + 1) * LANES)
                total = act[lane, at, :] + scale[:, lanes] * acc[at, lanes]
                act[lane, at, :] = total.astype(jnp.bfloat16).astype(jnp.float32)
            return inner

        lax.fori_loop(0, places * images // step_rows, add_rows, 0, unroll=4)
        return carry

    lax.fori_loop(0, sections, one_section, 0)

    def pool(place, total):
        at = pl.ds(pl.multiple_of(place * images, images), images)
        return tuple(part + act[lane, at, :] for lane, part in enumerate(total))

    start = (jnp.zeros((images, LANES), jnp.float32),) * (channels // LANES)
    pooled = lax.fori_loop(0, places, pool, start, unroll=8)
    pooled = jnp.concatenate(pooled, axis=1) * (1.0 / places)
    head = normalise(pooled, hgain_ref[...]).astype(jnp.bfloat16)
    proj[me] = jnp.dot(head, hproj_ref[...], preferred_element_type=jnp.float32).astype(
        jnp.bfloat16
    )
    swap = remote(proj.at[me], proj.at[me], proj_send, proj_recv)
    swap.start()

    def finish(c, carry):
        remote_in(me, c).wait_send()
        remote_out(me, c).wait_send()
        return carry

    remote_small(me).wait_send()
    lax.fori_loop(0, chunks, finish, 0)
    swap.wait_send()
    remote(proj.at[other], proj.at[other], proj_send, proj_recv).wait_recv()
    out_ref[...] = proj[...]


def tower(feats, small, w_in, w_out, head_gain, head_proj, taps):
    sections = lax.axis_size("pipe")
    images = feats.shape[0] // sections
    rows, cols, channels = feats.shape[1:]
    hidden = w_in.shape[1]
    width = head_proj.shape[1]
    chunks = hidden // CHUNK
    cells = rows * cols * images
    f32, b16 = jnp.float32, jnp.bfloat16
    dma = pltpu.SemaphoreType.DMA
    anywhere = pl.BlockSpec(memory_space=pl.ANY)
    vmem = pl.BlockSpec(memory_space=pltpu.VMEM)
    return pl.pallas_call(
        functools.partial(tower_kernel, taps),
        out_shape=jax.ShapeDtypeStruct((sections, images, width), b16),
        in_specs=[anywhere, anywhere, anywhere, anywhere, vmem, vmem],
        out_specs=vmem,
        scratch_shapes=[
            pltpu.VMEM((images, rows, cols, channels), b16),
            pltpu.VMEM((sections,) + small.shape, f32),
            pltpu.VMEM((sections, chunks, channels, CHUNK), b16),
            pltpu.VMEM((sections, chunks, CHUNK, channels), b16),
            pltpu.VMEM((channels // LANES, cells, LANES), f32),
            pltpu.VMEM((cells, channels), f32),
            pltpu.VMEM((cells, channels), b16),
            pltpu.VMEM((cells, channels), f32),
            pltpu.VMEM((cells, CHUNK), f32),
            pltpu.VMEM((cells, CHUNK), f32),
            pltpu.VMEM((taps * taps, images, LANES), f32),
            pltpu.VMEM((sections, images, width), b16),
            dma,
            dma((sections,)),
            dma((sections, chunks)),
            dma((sections, chunks)),
            dma,
            dma((chunks,)),
            dma((chunks,)),
            dma,
            dma,
        ],
        compiler_params=pltpu.CompilerParams(
            collective_id=0, has_side_effects=True, vmem_limit_bytes=52 << 20
        ),
        cost_estimate=pl.CostEstimate(
            flops=4 * sections * cells * channels * hidden,
            bytes_accessed=4 * channels * hidden * 4,
            transcendentals=sections * cells * hidden,
        ),
        name="tower",
    )(feats, small, w_in, w_out, head_gain, head_proj)


def pair_terms(unit_rows, match_rows, yield_rows, first_global, logit_scale, logit_bias):
    logits = (
        logit_scale * jnp.dot(unit_rows, yield_rows.T, preferred_element_type=jnp.float32)
        + logit_bias
    )
    columns = first_global + jnp.arange(yield_rows.shape[0], dtype=jnp.int32)
    label = jnp.where(match_rows[:, None] == columns[None, :], 1.0, -1.0).astype(jnp.float32)
    coef = (-label * logit_scale * jax.nn.sigmoid(-label * logits)).astype(jnp.bfloat16)
    return jnp.dot(coef, yield_rows, preferred_element_type=jnp.float32)


def on_device(
    feats,
    dw_kernel,
    ln_gain,
    w_in,
    w_out,
    layer_scale,
    head_gain,
    head_proj,
    yield_embeds,
    match_ids,
    logit_scale,
    logit_bias,
):
    segment = lax.axis_index("pipe")
    taps = dw_kernel.shape[1]
    channels = feats.shape[-1]
    gathered = lax.all_gather(yield_embeds, "dp", axis=0, tiled=True)
    used = taps * taps + 2
    small = jnp.concatenate(
        [
            dw_kernel[0].reshape(taps * taps, channels).astype(jnp.float32),
            ln_gain,
            layer_scale,
            jnp.zeros((-used % 8, channels), jnp.float32),
        ],
        axis=0,
    )
    projected = tower(
        feats, small, w_in[0], w_out[0], head_gain[None, :], head_proj, taps
    ).reshape(feats.shape[0], -1)
    wide = projected.astype(jnp.float32)
    unit = (wide / jnp.sqrt(jnp.sum(wide * wide, axis=-1, keepdims=True) + 1e-06)).astype(
        jnp.bfloat16
    )
    row_base = segment * lax.axis_size("dp") * yield_embeds.shape[0]
    partial_grad = pair_terms(unit, match_ids, gathered, row_base, logit_scale, logit_bias)
    embed_grad = lax.psum(partial_grad.astype(jnp.bfloat16), "pipe").astype(jnp.float32)
    return (projected, embed_grad)


def solution(mesh):
    in_specs = (
        P("dp", None, None, None),
        P("pipe", None, None, None),
        P("pipe", None),
        P("pipe", None, None),
        P("pipe", None, None),
        P("pipe", None),
        P(),
        P(),
        P(("pipe", "dp"), None),
        P("dp"),
        P(),
        P(),
    )
    out_specs = (P("dp", None), P("dp", None))
    return jax.shard_map(
        on_device, mesh=mesh, in_specs=in_specs, out_specs=out_specs, check_vma=False
    )
```

time: 368 us -> 89.2 us (0.24)
  other arithmetic: 178 us -> 0.83 us
  starting transfers between devices: 70.8 us -> 0.04 us
  matrix products: 62.8 us -> 3.19 us
  Pallas kernels: 0 us -> 36 us
  local copies, waits for them, and re-layouts: 29.4 us -> 4.82 us
  waiting for transfers between devices: 1.12 us -> 25.3 us
    reduce_sum x14 -> x0, other arithmetic: 149 us -> none  [the longest x5 142 us: layer_norm(): mean = jnp.mean(value, axis=-1, keepdims=True)]
    ppermute x5 -> x0, starting transfers between devices: 70.8 us -> none  [shifted(): lax.ppermute(value, axis, [(source, source + steps) for source in range(i...]
    dot_general x5 -> x0, matrix products: 59.6 us -> none  [the longest x4 58.5 us: block_batch(): branch = jnp.dot(hidden, weight_out, preferred_element_type=jnp.float32)]
    pallas_call x0 -> x1, Pallas kernels: none -> 36 us  [tower(): pl.pallas_call(functools.partial(tower_kernel, taps), out_shape=jax.Shape...]
    all_gather x1, waiting for transfers between devices: 0.02 us -> 24.6 us  [on_device(): gathered = lax.all_gather(yield_embeds, 'dp', axis=0, tiled=True)]
    convert_element_type x12 -> x0, other arithmetic: 18.3 us -> none  [the longest x4 10.1 us: block_batch(): result = act.reshape(-1, channels).astype(jnp.float32) + scale * branch]
    reshape x8 -> x0, local copies, waits for them, and re-layouts: 9.57 us -> none  [the longest x4 5.29 us: block_batch(): normed = layer_norm(conv, gain).astype(jnp.bfloat16).reshape(-1, channels)]
    select_n x5 -> x0, other arithmetic: 6.76 us -> none  [tick(): pooled = jnp.where(keep, updated, pooled)]
  transfers between devices with their start and end apart: 6 -> 1, of which waited for: 5 -> 1; matrix products, arithmetic and copies ran while one was open for 73% -> 5% of each run, Pallas kernels for 0% -> 40%
where the time goes in v1:
time: 89.2 us; the launch traced here: 89 us
  Pallas kernels  36 us (40%)
  waiting for transfers between devices  25.3 us (28%)
  between operations  15.5 us (17%)
  local copies, waits for them, and re-layouts  4.82 us (5%)
  blocking collectives  3.4 us (4%)
  matrix products  3.19 us (4%)
    pallas_call x1, Pallas kernels, tower(): pl.pallas_call(functools.partial(tower_kernel, taps), out_shape=jax.Shape...  36 us
    all_gather x1, waiting for transfers between devices, on_device(): gathered = lax.all_gather(yield_embeds, 'dp', axis=0, tiled=True)  24.6 us
    unnamed x14, local copies, waits for them, and re-layouts  4.62 us
    psum x1, blocking collectives, on_device(): lax.psum(partial_grad.astype(jnp.bfloat16), 'pipe').astype(jnp.float32)  3.4 us
    dot_general x1, matrix products, pair_terms(): return jnp.dot(coef, yield_rows, preferred_element_type=jnp.float32)  3.19 us
  transfers between devices with their start and end apart: 1, of which 1 were waited for; matrix products, arithmetic and copies ran while one was open for 5% of the time, Pallas kernels for 40%

profile of v1, /device:TPU:0, one launch (start us, length us, event | category | flops | bytes accessed | tf_op | source)
XLA Modules:
  0.0 89.0 jit_solution(10420817766118587123)
XLA Ops:
  7.2 0.0 all-gather.2.cloned.1.call-start
  7.2 0.7 all-gather.2.cloned.1.call-update
  7.9 0.0 copy-start.1
  7.9 0.0 copy-start.2
  7.9 0.0 copy-start.3
  7.9 0.0 copy-start.4
  7.9 0.0 copy-start
  8.0 4.0 %copy.14.feats_hbm = bf16[16,8,10,768]{3,2,1,0:T(8,128)(2,1)} copy(bf16[16,8,10,768]{3,1,2,0:T(8,128)(2,1)} %param.12) | data formatting | bytes 3932160 | tf_op args[0]
  11.9 0.0 copy-done.1
  12.0 0.0 copy-done.2
  12.0 0.1 pad.3.clone
  12.1 0.0 copy-done.3
  12.1 0.0 copy-done.4
  12.1 0.1 maximum_maximum_fusion.small_hbm
  12.2 0.0 copy-done
  12.2 0.0 copy-start.5
  12.2 36.0 %tower.1 = bf16[2,8,1024]{2,1,0:T(8,128)(2,1)S(1)} custom-call(bf16[16,8,10,768]{3,2,1,0:T(8,128)(2,1)} %copy.14.feats_hbm, f32[56,768]{1,0:T(8,128)S(1)} %maximum_maximum_fusion.small_hbm, bf16[768,3072]{1,0:T(8,128)(2,1)} %bitcast.7, bf16[3072,768]{1,0:T(8,128)(2,1)} %bitcast.8, f32[1,768]{1,0:T(1,128)S(1)} %broadcast_in_dim.18.hgain_ref, ...), custom_call_target="tpu_custom_call" | custom-call | flops 12079595520 | bytes 37748736 | tf_op jit(solution)/shard_map/tower/pallas_call | solution.py:293
  48.2 0.1 multiply_reduce_fusion
  48.3 0.1 sqrt.12
  49.7 24.6 %all-gather.2.cloned.1.call-done = bf16[1024,1024]{1,0:T(8,128)(2,1)} async-done(((bf16[64,1024]{1,0:T(8,128)(2,1)}), bf16[1024,1024]{1,0:T(8,128)(2,1)}) %all-gather.2.cloned.1.call-update) | async-done | bytes 2097168 | tf_op jit(solution)/shard_map/all_gather | solution.py:361
  74.3 3.2 %convolution_convert_fusion = bf16[16,1024]{1,0:T(8,128)(2,1)S(1)} fusion(bf16[1024,1024]{1,0:T(8,128)(2,1)} %all-gather.2.cloned.1.call-done, bf16[16,1024]{1,0:T(8,128)(2,1)S(1)} %bitcast.5, f32[]{:T(128)S(6)} %copy.17, f32[16]{0:T(128)S(1)} %sqrt.12, f32[]{:T(128)S(6)} %copy.16, s32[1024]{0:T(1024)S(1)} %iota_add_fusion, s32[16]{0:T(128)S(1)} %copy-done.5), kind=kOutput, calls=%fused_computation.8 | convolution fusion | flops 67371008 | bytes 2166920 | tf_op jit(solution)/shard_map/dot_general | solution.py:341
  77.5 3.4 %psum.7 = bf16[16,1024]{1,0:T(8,128)(2,1)S(1)} all-reduce(bf16[16,1024]{1,0:T(8,128)(2,1)S(1)} %convolution_convert_fusion), channel_id=1, replica_groups=mesh['pipe'=2,'dp'=16] {'pipe'}, use_global_device_ids=true, to_apply=%region_1.2 | all-reduce | flops 16384 | bytes 65536 | tf_op jit(solution)/shard_map/psum | solution.py:381
  80.9 0.6 convert_element_type.31
  81.5 0.6 copy.18
  (6 shorter events, 0.1 us)
Async XLA Ops:
  7.2 67.1 %all-gather.2.cloned.1.call-start = ((), (), s32[]{:S(2)}) async-start(), calls=%async_computation | async-start | bytes 2228224 | tf_op jit(solution)/shard_map/all_gather | solution.py:361
  7.9 4.0 %copy-start.1 = (bf16[1,7,7,768]{3,2,1,0:T(8,128)(2,1)S(1)}, bf16[1,7,7,768]{3,2,1,0:T(8,128)(2,1)}, u32[]{:S(2)}) copy-start(bf16[1,7,7,768]{3,2,1,0:T(8,128)(2,1)} %param.13) | copy-start | bytes 225796
  7.9 4.1 %copy-start.2 = (f32[768]{0:T(1024)S(1)}, f32[768]{0:T(1024)}, u32[]{:S(2)}) copy-start(f32[768]{0:T(1024)} %param.18) | copy-start | bytes 9220
  7.9 4.2 %copy-start.3 = (f32[1,768]{1,0:T(1,128)S(1)}, f32[1,768]{1,0:T(1,128)}, u32[]{:S(2)}) copy-start(f32[1,768]{1,0:T(1,128)} %param.17) | copy-start | bytes 9220
  7.9 4.2 %copy-start.4 = (f32[1,768]{1,0:T(1,128)S(1)}, f32[1,768]{1,0:T(1,128)}, u32[]{:S(2)}) copy-start(f32[1,768]{1,0:T(1,128)} %param.14) | copy-start | bytes 9220
  7.9 4.2 %copy-start = (bf16[768,1024]{1,0:T(8,128)(2,1)S(1)}, bf16[768,1024]{1,0:T(8,128)(2,1)}, u32[]{:S(2)}) copy-start(bf16[768,1024]{1,0:T(8,128)(2,1)} %hproj_ref.1) | copy-start | bytes 4718596
  12.2 62.1 %copy-start.5 = (s32[16]{0:T(128)S(1)}, s32[16]{0:T(128)}, u32[]{:S(2)}) copy-start(s32[16]{0:T(128)} %param.21) | copy-start | bytes 196
Sparse Core Ops, SparseCore 0:
  10.8 63.4 all-gather.1

commit v2 on v1

--- a/solution.py
+++ b/solution.py
@@ -38,13 +38,19 @@
 
 def tower_kernel(
     taps,
+    grid,
     feats_hbm,
     small_hbm,
     win_hbm,
     wout_hbm,
     hgain_ref,
     hproj_ref,
+    yields_hbm,
+    match_ref,
+    logit_scale_ref,
+    logit_bias_ref,
     out_ref,
+    grad_ref,
     feats,
     small,
     win,
@@ -57,6 +63,8 @@
     raw_b,
     wide_taps,
     proj,
+    pool_y,
+    grads,
     feat_sem,
     small_sem,
     in_sem,
@@ -66,8 +74,17 @@
     out_send,
     proj_send,
     proj_recv,
+    grad_send,
+    grad_recv,
+    own_sem,
+    z_send,
+    z_recv,
+    x_send,
+    x_recv,
+    y_send,
+    y_recv,
 ):
-    images, rows, cols, channels = feats.shape
+    images, cols, rows, channels = feats.shape
     sections = win.shape[0]
     chunks = win.shape[1]
     places = rows * cols
@@ -110,15 +127,140 @@
     def remote_out(section, c):
         return remote(out_source(c), wout.at[section, c], out_send.at[c], out_sem.at[section, c])
 
+    deep, tall, wide = grid
+    place = lax.axis_index("dp")
+    at_z = place // (tall * wide)
+    at_y = place // wide % tall
+    at_x = place % wide
+
+    def chip(z, y, x):
+        return {"dp": (z * tall + y) * wide + x}
+
+    def remote_to(source, target, send, recv, device):
+        return pltpu.make_async_remote_copy(
+            src_ref=source,
+            dst_ref=target,
+            send_sem=send,
+            recv_sem=recv,
+            device_id=device,
+            device_id_type=pl.DeviceIdType.MESH,
+        )
+
+    def turn(value, step, count):
+        return lax.rem(value + step, count)
+
+    def z_copy(step):
+        return remote_to(
+            yields_hbm,
+            pool_y.at[at_z, at_y, at_x],
+            z_send.at[step],
+            z_recv.at[step],
+            chip(turn(at_z, step, deep), at_y, at_x),
+        )
+
+    def x_copy(step, half, second):
+        part = pool_y.at[:, :, at_x, half] if second else pool_y.at[:, at_y, at_x, half]
+        return remote_to(
+            part,
+            part,
+            x_send.at[half, step],
+            x_recv.at[half, step],
+            chip(at_z, at_y, turn(at_x, step, wide)),
+        )
+
+    def y_copy(step, half, second):
+        part = pool_y.at[:, at_y, :, half] if second else pool_y.at[:, at_y, at_x, half]
+        return remote_to(
+            part,
+            part,
+            y_send.at[half, step],
+            y_recv.at[half, step],
+            chip(at_z, turn(at_y, step, tall), at_x),
+        )
+
+    def x_arrival(step, half, second):
+        source = turn(at_x, wide - step, wide)
+        part = pool_y.at[:, :, source, half] if second else pool_y.at[:, at_y, source, half]
+        return remote_to(
+            part, part, x_send.at[half, step], x_recv.at[half, step], chip(at_z, at_y, source)
+        )
+
+    def y_arrival(step, half, second):
+        source = turn(at_y, tall - step, tall)
+        part = pool_y.at[:, source, :, half] if second else pool_y.at[:, source, at_x, half]
+        return remote_to(
+            part, part, y_send.at[half, step], y_recv.at[half, step], chip(at_z, source, at_x)
+        )
+
+    def z_arrival(step):
+        source = turn(at_z, deep - step, deep)
+        return remote_to(
+            yields_hbm,
+            pool_y.at[source, at_y, at_x],
+            z_send.at[step],
+            z_recv.at[step],
+            chip(source, at_y, at_x),
+        )
+
+    own_yields = pltpu.make_async_copy(yields_hbm, pool_y.at[at_z, at_y, at_x], own_sem)
+
+    def gather_begin():
+        for step in range(1, deep):
+            z_copy(step).start()
+        own_yields.start()
+
+    def gather_second():
+        own_yields.wait()
+        for step in range(1, deep):
+            z_arrival(step).wait_recv()
+        for step in range(1, wide):
+            x_copy(step, 0, False).start()
+        for step in range(1, tall):
+            y_copy(step, 1, False).start()
+
+    def gather_third():
+        for step in range(1, wide):
+            x_arrival(step, 0, False).wait_recv()
+        for step in range(1, tall):
+            y_arrival(step, 1, False).wait_recv()
+        for step in range(1, tall):
+            y_copy(step, 0, True).start()
+        for step in range(1, wide):
+            x_copy(step, 1, True).start()
+
+    def gather_end():
+        for step in range(1, tall):
+            y_arrival(step, 0, True).wait_recv()
+        for step in range(1, wide):
+            x_arrival(step, 1, True).wait_recv()
+        for step in range(1, deep):
+            z_copy(step).wait_send()
+        for step in range(1, wide):
+            x_copy(step, 0, False).wait_send()
+            x_copy(step, 1, True).wait_send()
+        for step in range(1, tall):
+            y_copy(step, 1, False).wait_send()
+            y_copy(step, 0, True).wait_send()
+
     fetch = pltpu.make_async_copy(feats_hbm.at[pl.ds(me * images, images)], feats, feat_sem)
     fetch.start()
     local_small().start()
 
     barrier = pltpu.get_barrier_semaphore()
     pl.semaphore_signal(barrier, inc=1, device_id=peer, device_id_type=pl.DeviceIdType.MESH)
-    pl.semaphore_wait(barrier, 1)
+    neighbours = (
+        [chip(turn(at_z, step, deep), at_y, at_x) for step in range(1, deep)]
+        + [chip(at_z, turn(at_y, step, tall), at_x) for step in range(1, tall)]
+        + [chip(at_z, at_y, turn(at_x, step, wide)) for step in range(1, wide)]
+    )
+    for neighbour in neighbours:
+        pl.semaphore_signal(
+            barrier, inc=1, device_id=neighbour, device_id_type=pl.DeviceIdType.MESH
+        )
+    pl.semaphore_wait(barrier, 1 + len(neighbours))
 
     remote_small(me).start()
+    gather_begin()
 
     def begin(c, carry):
         remote_in(me, c).start()
@@ -151,17 +293,13 @@
 
     fetch.wait()
 
-    def spread(image, carry):
-        for r in range(rows):
-            line = feats[image, r].astype(jnp.float32)
+    for image in range(images):
+        for w in range(cols):
+            line = feats[image, w].astype(jnp.float32)
             for block in range(channels // LANES):
-                act[block, pl.ds(r * cols * images + image, cols, stride=images), :] = line[
+                act[block, pl.ds(w * rows * images + image, rows, stride=images), :] = line[
                     :, block * LANES : (block + 1) * LANES
                 ]
-        return carry
-
-    for image in range(images):
-        spread(image, 0)
 
     def one_section(section, carry):
         await_small(section)
@@ -178,7 +316,7 @@
                         continue
                     kernel = [wide_taps[dy * taps + dx] for dx in range(taps)]
                     line = [
-                        act[block, pl.ds((source * cols + w) * images, images), :]
+                        act[block, pl.ds((w * rows + source) * images, images), :]
                         for w in range(cols)
                     ]
                     for w in range(cols):
@@ -189,7 +327,7 @@
                             term = line[at] * kernel[dx]
                             total[w] = term if total[w] is None else total[w] + term
                 for w in range(cols):
-                    conv[pl.ds((r * cols + w) * images, images), lanes] = total[w]
+                    conv[pl.ds((w * rows + r) * images, images), lanes] = total[w]
             return inner
 
         lax.fori_loop(0, channels // LANES, conv_lanes, 0)
@@ -212,6 +350,10 @@
             first = 2 * j
             after = jnp.minimum(first + 2, chunks - 1)
             await_chunk(section, first + 1)
+
+            @pl.when(jnp.logical_and(section == 0, j == chunks // 4))
+            def _():
+                gather_second()
 
             @pl.when(first + 2 < chunks)
             def _():
@@ -248,6 +390,11 @@
             return inner
 
         lax.fori_loop(0, places * images // step_rows, add_rows, 0, unroll=4)
+
+        @pl.when(section == 0)
+        def _():
+            gather_third()
+
         return carry
 
     lax.fori_loop(0, sections, one_section, 0)
@@ -266,6 +413,8 @@
     swap = remote(proj.at[me], proj.at[me], proj_send, proj_recv)
     swap.start()
 
+    gather_end()
+
     def finish(c, carry):
         remote_in(me, c).wait_send()
         remote_out(me, c).wait_send()
@@ -277,26 +426,69 @@
     remote(proj.at[other], proj.at[other], proj_send, proj_recv).wait_recv()
     out_ref[...] = proj[...]
 
-
-def tower(feats, small, w_in, w_out, head_gain, head_proj, taps):
+    count = sections * images
+    width = proj.shape[-1]
+    projected = proj[...].astype(jnp.float32).reshape(count, width)
+    length = jnp.sqrt(jnp.sum(projected * projected, axis=-1, keepdims=True) + 1e-06)
+    unit = (projected / length).astype(jnp.bfloat16)
+    logit_scale = logit_scale_ref[0]
+    logit_bias = logit_bias_ref[0]
+    match = match_ref[...]
+    held = tall * wide * yields_hbm.shape[0] * yields_hbm.shape[1]
+
+    def pairs(z, total):
+        yields = pool_y[z].reshape(held, width)
+        dots = lax.dot_general(
+            unit, yields, (((1,), (1,)), ((), ())), preferred_element_type=jnp.float32
+        )
+        logits = logit_scale * dots + logit_bias
+        first = (me * deep + z) * held
+        columns = first + lax.broadcasted_iota(jnp.int32, (count, held), 1)
+        label = jnp.where(match == columns, 1.0, -1.0)
+        coef = (-label * logit_scale * jax.nn.sigmoid(-label * logits)).astype(jnp.bfloat16)
+        return total + jnp.dot(coef, yields, preferred_element_type=jnp.float32)
+
+    grads[me] = lax.fori_loop(
+        0, deep, pairs, jnp.zeros((count, width), jnp.float32), unroll=min(deep, 4)
+    )
+    trade = remote(grads.at[me], grads.at[me], grad_send, grad_recv)
+    trade.start()
+    trade.wait_send()
+    remote(grads.at[other], grads.at[other], grad_send, grad_recv).wait_recv()
+    grad_ref[...] = grads[0] + grads[1]
+
+
+def chip_grid(count):
+    side = 1
+    while 2 * side**3 < count:
+        side += 1
+    return (2 * side, side, side) if 2 * side**3 == count else (count, 1, 1)
+
+
+def tower(feats, small, w_in, w_out, head_gain, head_proj, yields, match, scale, bias, taps):
     sections = lax.axis_size("pipe")
     images = feats.shape[0] // sections
-    rows, cols, channels = feats.shape[1:]
+    cols, rows, channels = feats.shape[1:]
     hidden = w_in.shape[1]
     width = head_proj.shape[1]
     chunks = hidden // CHUNK
     cells = rows * cols * images
+    grid = chip_grid(lax.axis_size("dp"))
     f32, b16 = jnp.float32, jnp.bfloat16
     dma = pltpu.SemaphoreType.DMA
     anywhere = pl.BlockSpec(memory_space=pl.ANY)
     vmem = pl.BlockSpec(memory_space=pltpu.VMEM)
+    smem = pl.BlockSpec(memory_space=pltpu.SMEM)
     return pl.pallas_call(
-        functools.partial(tower_kernel, taps),
-        out_shape=jax.ShapeDtypeStruct((sections, images, width), b16),
-        in_specs=[anywhere, anywhere, anywhere, anywhere, vmem, vmem],
-        out_specs=vmem,
+        functools.partial(tower_kernel, taps, grid),
+        out_shape=(
+            jax.ShapeDtypeStruct((sections, images, width), b16),
+            jax.ShapeDtypeStruct((sections * images, width), f32),
+        ),
+        in_specs=[anywhere] * 4 + [vmem, vmem, anywhere, vmem, smem, smem],
+        out_specs=(vmem, vmem),
         scratch_shapes=[
-            pltpu.VMEM((images, rows, cols, channels), b16),
+            pltpu.VMEM((images, cols, rows, channels), b16),
             pltpu.VMEM((sections,) + small.shape, f32),
             pltpu.VMEM((sections, chunks, channels, CHUNK), b16),
             pltpu.VMEM((sections, chunks, CHUNK, channels), b16),
@@ -308,6 +500,8 @@
             pltpu.VMEM((cells, CHUNK), f32),
             pltpu.VMEM((taps * taps, images, LANES), f32),
             pltpu.VMEM((sections, images, width), b16),
+            pltpu.VMEM(grid + yields.shape, b16),
+            pltpu.VMEM((sections, sections * images, width), f32),
             dma,
             dma((sections,)),
             dma((sections, chunks)),
@@ -317,9 +511,18 @@
             dma((chunks,)),
             dma,
             dma,
+            dma,
+            dma,
+            dma,
+            dma((grid[0],)),
+            dma((grid[0],)),
+            dma((2, grid[2])),
+            dma((2, grid[2])),
+            dma((2, grid[1])),
+            dma((2, grid[1])),
         ],
         compiler_params=pltpu.CompilerParams(
-            collective_id=0, has_side_effects=True, vmem_limit_bytes=52 << 20
+            collective_id=0, has_side_effects=True, vmem_limit_bytes=58 << 20
         ),
         cost_estimate=pl.CostEstimate(
             flops=4 * sections * cells * channels * hidden,
@@ -327,18 +530,7 @@
             transcendentals=sections * cells * hidden,
         ),
         name="tower",
-    )(feats, small, w_in, w_out, head_gain, head_proj)
-
-
-def pair_terms(unit_rows, match_rows, yield_rows, first_global, logit_scale, logit_bias):
-    logits = (
-        logit_scale * jnp.dot(unit_rows, yield_rows.T, preferred_element_type=jnp.float32)
-        + logit_bias
-    )
-    columns = first_global + jnp.arange(yield_rows.shape[0], dtype=jnp.int32)
-    label = jnp.where(match_rows[:, None] == columns[None, :], 1.0, -1.0).astype(jnp.float32)
-    coef = (-label * logit_scale * jax.nn.sigmoid(-label * logits)).astype(jnp.bfloat16)
-    return jnp.dot(coef, yield_rows, preferred_element_type=jnp.float32)
+    )(feats, small, w_in, w_out, head_gain, head_proj, yields, match, scale, bias)
 
 
 def on_device(
@@ -355,10 +547,8 @@
     logit_scale,
     logit_bias,
 ):
-    segment = lax.axis_index("pipe")
     taps = dw_kernel.shape[1]
     channels = feats.shape[-1]
-    gathered = lax.all_gather(yield_embeds, "dp", axis=0, tiled=True)
     used = taps * taps + 2
     small = jnp.concatenate(
         [
@@ -369,17 +559,20 @@
         ],
         axis=0,
     )
-    projected = tower(
-        feats, small, w_in[0], w_out[0], head_gain[None, :], head_proj, taps
-    ).reshape(feats.shape[0], -1)
-    wide = projected.astype(jnp.float32)
-    unit = (wide / jnp.sqrt(jnp.sum(wide * wide, axis=-1, keepdims=True) + 1e-06)).astype(
-        jnp.bfloat16
-    )
-    row_base = segment * lax.axis_size("dp") * yield_embeds.shape[0]
-    partial_grad = pair_terms(unit, match_ids, gathered, row_base, logit_scale, logit_bias)
-    embed_grad = lax.psum(partial_grad.astype(jnp.bfloat16), "pipe").astype(jnp.float32)
-    return (projected, embed_grad)
+    projected, embed_grad = tower(
+        feats.transpose(0, 2, 1, 3),
+        small,
+        w_in[0],
+        w_out[0],
+        head_gain[None, :],
+        head_proj,
+        yield_embeds.reshape(2, yield_embeds.shape[0] // 2, yield_embeds.shape[1]),
+        match_ids[:, None],
+        logit_scale[None],
+        logit_bias[None],
+        taps,
+    )
+    return (projected.reshape(feats.shape[0], -1), embed_grad)
 
 
 def solution(mesh):

time: 89.2 us -> 58.3 us (0.65)
  waiting for transfers between devices: 25.3 us -> 0 us
  between operations: 15.5 us -> 1.95 us
  Pallas kernels: 36 us -> 48 us
  blocking collectives: 3.4 us -> 0 us
  matrix products: 3.19 us -> 0 us
  local copies, waits for them, and re-layouts: 4.82 us -> 6.44 us
    all_gather x1 -> x0, waiting for transfers between devices: 24.6 us -> none  [on_device(): gathered = lax.all_gather(yield_embeds, 'dp', axis=0, tiled=True)]
    pallas_call x1, Pallas kernels: 36 us -> 48 us  [tower(): pl.pallas_call(functools.partial(tower_kernel, taps, grid), out_shape=(ja...]
    psum x1 -> x0, blocking collectives: 3.4 us -> none  [on_device(): lax.psum(partial_grad.astype(jnp.bfloat16), 'pipe').astype(jnp.float32)]
    dot_general x1 -> x0, matrix products: 3.19 us -> none  [pair_terms(): return jnp.dot(coef, yield_rows, preferred_element_type=jnp.float32)]
    unnamed x14 -> x2, local copies, waits for them, and re-layouts: 4.62 us -> 2.85 us
    concatenate x1, other arithmetic: 0.08 us -> 1.45 us  [on_device(): jnp.concatenate([dw_kernel[0].reshape(taps * taps, channels).astype(jnp.f...]
    broadcast_in_dim x0 -> x1, local copies, waits for them, and re-layouts: none -> 1.33 us  [on_device(): match_ids[:, None]]
    broadcast_in_dim x1, local copies, waits for them, and re-layouts: 0.01 us -> 1.27 us  [on_device(): head_gain[None, :]]
  transfers between devices with their start and end apart: 1 -> 0, of which waited for: 1 -> 0; matrix products, arithmetic and copies ran while one was open for 5% -> 0% of each run, Pallas kernels for 40% -> 0%
where the time goes in v2:
time: 58.3 us; the launch traced here: 57.9 us
  Pallas kernels  48 us (82%)
  local copies, waits for them, and re-layouts  6.44 us (11%)
  between operations  1.95 us (3%)
  other arithmetic  1.45 us (2%)
    pallas_call x1, Pallas kernels, tower(): pl.pallas_call(functools.partial(tower_kernel, taps, grid), out_shape=(ja...  48 us
    unnamed x2, local copies, waits for them, and re-layouts  2.85 us
    concatenate x1, other arithmetic, on_device(): jnp.concatenate([dw_kernel[0].reshape(taps * taps, channels).astype(jnp.f...  1.45 us
    broadcast_in_dim x1, local copies, waits for them, and re-layouts, on_device(): match_ids[:, None]  1.33 us
    broadcast_in_dim x1, local copies, waits for them, and re-layouts, on_device(): head_gain[None, :]  1.27 us

profile of v2, /device:TPU:0, one launch (start us, length us, event | category | flops | bytes accessed | tf_op | source)
XLA Modules:
  0.0 57.9 jit_solution(5716172237851487456)
XLA Ops:
  0.6 0.9 %reshape.14 = f32[49,768]{1,0:T(8,128)S(1)} reshape(bf16[1,7,7,768]{3,2,1,0:T(8,128)(2,1)} %param.13) | data formatting | bytes 225792 | tf_op jit(solution)/shard_map/convert_element_type | solution.py:555
  1.6 0.1 pad.3.clone
  1.6 1.4 %maximum_maximum_fusion.small_hbm = f32[56,768]{1,0:T(8,128)} fusion(f32[1,768]{1,0:T(1,128)} %param.17, f32[1,768]{1,0:T(1,128)} %param.14, f32[49,768]{1,0:T(8,128)S(1)} %reshape.14, f32[56]{0:T(128)S(1)} %pad.3.clone), kind=kLoop, calls=%fused_computation | loop fusion | flops 129024 | bytes 328928 | tf_op jit(solution)/shard_map/concatenate | solution.py:553
  3.1 1.3 %copy.14.match_ref = s32[16,1]{1,0:T(8,128)} copy(s32[16,1]{0,1:T(1,128)} %bitcast.11) | data formatting | bytes 128 | tf_op jit(solution)/shard_map/broadcast_in_dim | solution.py:570
  4.4 1.3 %broadcast_in_dim.16.hgain_ref = f32[1,768]{1,0:T(1,128)} reshape(f32[768]{0:T(1024)} %param.18) | data formatting | bytes 6144 | tf_op jit(solution)/shard_map/broadcast_in_dim | solution.py:567
  7.0 48.0 %tower.1 = (bf16[2,8,1024]{2,1,0:T(8,128)(2,1)}, f32[16,1024]{1,0:T(8,128)}) custom-call(bf16[16,10,8,768]{3,2,1,0:T(8,128)(2,1)} %bitcast.14, f32[56,768]{1,0:T(8,128)} %maximum_maximum_fusion.small_hbm, bf16[768,3072]{1,0:T(8,128)(2,1)} %bitcast.12, bf16[3072,768]{1,0:T(8,128)(2,1)} %bitcast.13, f32[1,768]{1,0:T(1,128)} %broadcast_in_dim.16.hgain_ref, ...), custom_call_target="tpu_custom_call" | custom-call | flops 12079595520 | bytes 37748736 | tf_op jit(solution)/shard_map/tower/pallas_call | solution.py:482
  55.0 1.4 %copy.19 = bf16[16,1024]{1,0:T(8,128)(2,1)} copy(bf16[16,1024]{1,0:T(8,128)(2,1)} %bitcast.10) | data formatting | bytes 65536
  56.4 1.5 %copy.20 = f32[16,1024]{1,0:T(8,128)} copy(f32[16,1024]{1,0:T(8,128)} %get-tuple-element.9) | data formatting | bytes 131072
  (1 shorter events, 0.0 us)

commit v3 on v2

--- a/solution.py
+++ b/solution.py
@@ -7,7 +7,7 @@
 from jax.experimental.pallas import tpu as pltpu
 from jax.sharding import PartitionSpec as P
 
-CHUNK = 256
+CHUNK = 512
 LANES = 128
 ERF_POLY = (
     7.97872669e-01,
@@ -344,40 +344,39 @@
 
         acc[...] = jnp.zeros_like(acc)
         await_chunk(section, 0)
-        raw_a[...] = jnp.dot(normed[...], win[section, 0], preferred_element_type=jnp.float32)
-
-        def pair(j, inner):
+
+        def enter(c):
+            out = jnp.dot(normed[...], win[section, c], preferred_element_type=jnp.float32)
+            return out.astype(raw_a.dtype)
+
+        def leave(source, c):
+            hidden = gelu(source[...]).astype(jnp.bfloat16)
+            return jnp.dot(hidden, wout[section, c], preferred_element_type=jnp.float32)
+
+        raw_a[...] = enter(0)
+
+        def pair(j, more):
             first = 2 * j
-            after = jnp.minimum(first + 2, chunks - 1)
             await_chunk(section, first + 1)
 
             @pl.when(jnp.logical_and(section == 0, j == chunks // 4))
             def _():
                 gather_second()
 
-            @pl.when(first + 2 < chunks)
-            def _():
-                await_chunk(section, after)
-
-            raw_b[...] = jnp.dot(
-                normed[...], win[section, first + 1], preferred_element_type=jnp.float32
-            )
-            acc[...] += jnp.dot(
-                gelu(raw_a[...]).astype(jnp.bfloat16),
-                wout[section, first],
-                preferred_element_type=jnp.float32,
-            )
-            raw_a[...] = jnp.dot(
-                normed[...], win[section, after], preferred_element_type=jnp.float32
-            )
-            acc[...] += jnp.dot(
-                gelu(raw_b[...]).astype(jnp.bfloat16),
-                wout[section, first + 1],
-                preferred_element_type=jnp.float32,
-            )
+            if more:
+                await_chunk(section, first + 2)
+            raw_b[...] = enter(first + 1)
+            acc[...] += leave(raw_a, first)
+            if more:
+                raw_a[...] = enter(first + 2)
+            acc[...] += leave(raw_b, first + 1)
+
+        def pair_step(j, inner):
+            pair(j, True)
             return inner
 
-        lax.fori_loop(0, chunks // 2, pair, 0)
+        lax.fori_loop(0, chunks // 2 - 1, pair_step, 0)
+        pair(chunks // 2 - 1, False)
 
         scale = small[section, pl.ds(taps * taps + 1, 1), :]
 
@@ -474,6 +473,7 @@
     chunks = hidden // CHUNK
     cells = rows * cols * images
     grid = chip_grid(lax.axis_size("dp"))
+    deep_bytes = 2 * lax.axis_size("dp") * yields.size
     f32, b16 = jnp.float32, jnp.bfloat16
     dma = pltpu.SemaphoreType.DMA
     anywhere = pl.BlockSpec(memory_space=pl.ANY)
@@ -496,8 +496,8 @@
             pltpu.VMEM((cells, channels), f32),
             pltpu.VMEM((cells, channels), b16),
             pltpu.VMEM((cells, channels), f32),
-            pltpu.VMEM((cells, CHUNK), f32),
-            pltpu.VMEM((cells, CHUNK), f32),
+            pltpu.VMEM((cells, CHUNK), b16),
+            pltpu.VMEM((cells, CHUNK), b16),
             pltpu.VMEM((taps * taps, images, LANES), f32),
             pltpu.VMEM((sections, images, width), b16),
             pltpu.VMEM(grid + yields.shape, b16),
@@ -522,7 +522,7 @@
             dma((2, grid[1])),
         ],
         compiler_params=pltpu.CompilerParams(
-            collective_id=0, has_side_effects=True, vmem_limit_bytes=58 << 20
+            collective_id=0, has_side_effects=True, vmem_limit_bytes=(36 << 20) + deep_bytes
         ),
         cost_estimate=pl.CostEstimate(
             flops=4 * sections * cells * channels * hidden,

time: 58.3 us -> 57 us (0.978)
  Pallas kernels: 48 us -> 41.7 us
  local copies, waits for them, and re-layouts: 6.44 us -> 12.2 us
  other arithmetic: 1.45 us -> 0.78 us
    unnamed x2 -> x12, local copies, waits for them, and re-layouts: 2.85 us -> 9.77 us
    pallas_call x1, Pallas kernels: 48 us -> 41.7 us  [tower(): pl.pallas_call(functools.partial(tower_kernel, taps, grid), out_shape=(ja...]
    concatenate x1, other arithmetic: 1.45 us -> 0.78 us  [on_device(): jnp.concatenate([dw_kernel[0].reshape(taps * taps, channels).astype(jnp.f...]
    broadcast_in_dim x1, local copies, waits for them, and re-layouts: 1.33 us -> 0.73 us  [on_device(): match_ids[:, None]]
where the time goes in v3:
time: 57 us; the launch traced here: 56.6 us
  Pallas kernels  41.7 us (73%)
  local copies, waits for them, and re-layouts  12.2 us (21%)
  between operations  1.96 us (3%)
  other arithmetic  0.78 us (1%)
    pallas_call x1, Pallas kernels, tower(): pl.pallas_call(functools.partial(tower_kernel, taps, grid), out_shape=(ja...  41.7 us
    unnamed x12, local copies, waits for them, and re-layouts  9.77 us

profile of v3, /device:TPU:0, one launch (start us, length us, event | category | flops | bytes accessed | tf_op | source)
XLA Modules:
  0.0 56.6 jit_solution(4872193388354953547)
XLA Ops:
  0.6 0.9 %reshape.14 = f32[49,768]{1,0:T(8,128)S(1)} reshape(bf16[1,7,7,768]{3,2,1,0:T(8,128)(2,1)} %param.13) | data formatting | bytes 225792 | tf_op jit(solution)/shard_map/convert_element_type | solution.py:555
  1.6 0.1 pad.3.clone
  1.6 0.8 %maximum_maximum_fusion.small_hbm = f32[56,768]{1,0:T(8,128)S(1)} fusion(f32[1,768]{1,0:T(1,128)} %param.17, f32[1,768]{1,0:T(1,128)} %param.14, f32[49,768]{1,0:T(8,128)S(1)} %reshape.14, f32[56]{0:T(128)S(1)} %pad.3.clone), kind=kLoop, calls=%fused_computation | loop fusion | flops 129024 | bytes 328928 | tf_op jit(solution)/shard_map/concatenate | solution.py:553
  2.4 0.7 %copy.14.match_ref = s32[16,1]{1,0:T(8,128)S(1)} copy(s32[16,1]{0,1:T(1,128)} %bitcast.15) | data formatting | bytes 128 | tf_op jit(solution)/shard_map/broadcast_in_dim | solution.py:570
  3.2 0.7 %broadcast_in_dim.16.hgain_ref = f32[1,768]{1,0:T(1,128)S(1)} reshape(f32[768]{0:T(1024)} %param.18) | data formatting | bytes 6144 | tf_op jit(solution)/shard_map/broadcast_in_dim | solution.py:567
  5.1 0.0 copy-start
  5.2 2.3 %copy-done = bf16[1,768,3072]{2,1,0:T(8,128)(2,1)S(1)} copy-done((bf16[1,768,3072]{2,1,0:T(8,128)(2,1)S(1)}, bf16[1,768,3072]{2,1,0:T(8,128)(2,1)}, u32[]{:S(2)}) %copy-start) | copy-done | bytes 4718616
  7.5 0.0 copy-start.1
  7.5 2.3 %copy-done.1 = bf16[1,3072,768]{2,1,0:T(8,128)(2,1)S(1)} copy-done((bf16[1,3072,768]{2,1,0:T(8,128)(2,1)S(1)}, bf16[1,3072,768]{2,1,0:T(8,128)(2,1)}, u32[]{:S(2)}) %copy-start.1) | copy-done | bytes 4718616
  9.8 0.0 copy-start.2
  9.8 1.5 %copy-done.2 = bf16[16,8,10,768]{3,1,2,0:T(8,128)(2,1)S(1)} copy-done((bf16[16,8,10,768]{3,1,2,0:T(8,128)(2,1)S(1)}, bf16[16,8,10,768]{3,1,2,0:T(8,128)(2,1)}, u32[]{:S(2)}) %copy-start.2) | copy-done | bytes 1966104
  11.4 0.0 copy-start.3
  11.4 1.4 %copy-done.3 = bf16[768,1024]{1,0:T(8,128)(2,1)S(1)} copy-done((bf16[768,1024]{1,0:T(8,128)(2,1)S(1)}, bf16[768,1024]{1,0:T(8,128)(2,1)}, u32[]{:S(2)}) %copy-start.3) | copy-done | bytes 1572888
  12.8 0.0 copy-start.4
  12.8 0.9 %copy-done.4 = bf16[64,1024]{1,0:T(8,128)(2,1)S(1)} copy-done((bf16[64,1024]{1,0:T(8,128)(2,1)S(1)}, bf16[64,1024]{1,0:T(8,128)(2,1)}, u32[]{:S(2)}) %copy-start.4) | copy-done | bytes 131096
  13.7 41.7 %tower.1 = (bf16[2,8,1024]{2,1,0:T(8,128)(2,1)S(1)}, f32[16,1024]{1,0:T(8,128)S(1)}) custom-call(bf16[16,10,8,768]{3,2,1,0:T(8,128)(2,1)S(1)} %bitcast.13, f32[56,768]{1,0:T(8,128)S(1)} %maximum_maximum_fusion.small_hbm, bf16[768,3072]{1,0:T(8,128)(2,1)S(1)} %bitcast.11, bf16[3072,768]{1,0:T(8,128)(2,1)S(1)} %bitcast.12, ...), custom_call_target="tpu_custom_call" | custom-call | flops 12079595520 | bytes 37748736 | tf_op jit(solution)/shard_map/tower/pallas_call | solution.py:482
  55.4 0.6 %copy.19 = bf16[16,1024]{1,0:T(8,128)(2,1)} copy(bf16[16,1024]{1,0:T(8,128)(2,1)S(1)} %bitcast.10) | data formatting | bytes 65536
  56.0 0.6 %copy.20 = f32[16,1024]{1,0:T(8,128)} copy(f32[16,1024]{1,0:T(8,128)S(1)} %get-tuple-element.9) | data formatting | bytes 131072
  (1 shorter events, 0.0 us)
Async XLA Ops:
  5.1 2.3 %copy-start = (bf16[1,768,3072]{2,1,0:T(8,128)(2,1)S(1)}, bf16[1,768,3072]{2,1,0:T(8,128)(2,1)}, u32[]{:S(2)}) copy-start(bf16[1,768,3072]{2,1,0:T(8,128)(2,1)} %param.15) | copy-start | bytes 14155780
  7.5 2.3 %copy-start.1 = (bf16[1,3072,768]{2,1,0:T(8,128)(2,1)S(1)}, bf16[1,3072,768]{2,1,0:T(8,128)(2,1)}, u32[]{:S(2)}) copy-start(bf16[1,3072,768]{2,1,0:T(8,128)(2,1)} %param.16) | copy-start | bytes 14155780
  9.8 1.5 %copy-start.2 = (bf16[16,8,10,768]{3,1,2,0:T(8,128)(2,1)S(1)}, bf16[16,8,10,768]{3,1,2,0:T(8,128)(2,1)}, u32[]{:S(2)}) copy-start(bf16[16,8,10,768]{3,1,2,0:T(8,128)(2,1)} %param.12) | copy-start | bytes 5898244
  11.4 1.4 %copy-start.3 = (bf16[768,1024]{1,0:T(8,128)(2,1)S(1)}, bf16[768,1024]{1,0:T(8,128)(2,1)}, u32[]{:S(2)}) copy-start(bf16[768,1024]{1,0:T(8,128)(2,1)} %hproj_ref.1) | copy-start | bytes 4718596
  12.8 0.9 %copy-start.4 = (bf16[64,1024]{1,0:T(8,128)(2,1)S(1)}, bf16[64,1024]{1,0:T(8,128)(2,1)}, u32[]{:S(2)}) copy-start(bf16[64,1024]{1,0:T(8,128)(2,1)} %param.20) | copy-start | bytes 393220
